TPU v7x, 256 devices: a whole 4x4x8 slice. The times are simulated.
256 devices in a mesh: tok: 16 (over y, x), col: 16 (over z, core).
Axes of the slice: x: 4, y: 4, z: 8, core: 2. Of those that a mesh axis runs over, the one named last changes fastest.
Arguments:
- activations: bfloat16 [32768, 8192], P('tok', 'col'), may hold values from -60 to 60, as said below
- weight: bfloat16 [8192, 8192], P('tok', 'col'), may hold values from -6 to 6
- keep_mask: int32 [8192, 8192], P('tok', 'col'), may hold values from 0 to 1
Outputs:
- new_weight: bfloat16 [8192, 8192], P('tok', 'col')
Inputs may be any that keep to these rules, and one draw needn't show every extreme that they name: activations of calibration tokens.
All inputs are finite; a program needn't handle non-finite values.
Results may differ from a plain program's by a relative error of at most 0.00115.
Values may be sent and summed in bfloat16 or wider, within the bound.
A program may use at most 64 MiB of HBM per device.

v0:
```python
import jax
import jax.numpy as jnp
from jax import lax
from jax.sharding import PartitionSpec as P

B = 1024
ITERS = 4


def split(x):
    high = lax.reduce_precision(x, exponent_bits=8, mantissa_bits=7)
    return (high.astype(jnp.bfloat16), (x - high).astype(jnp.bfloat16))


def mm(a, b, dims=(((1,), (0,)), ((), ()))):
    return lax.dot_general(a, b, dims, preferred_element_type=jnp.float32)


def per_device(activations, weight, keep_mask):
    n_col = lax.axis_size("col")
    n_tok = lax.axis_size("tok")
    tok_rows = activations.shape[0]
    panel_width = B // n_col
    total_count = tok_rows * n_tok
    pruned = jnp.where(
        keep_mask[:, :panel_width] == 0, weight[:, :panel_width], jnp.zeros((), jnp.bfloat16)
    )
    panel = lax.all_gather(activations[:, :panel_width], "col", axis=1, tiled=True)
    partial_panel = mm(activations, panel, (((0,), (0,)), ((), ())))
    pruned_panel = lax.all_gather(pruned, "col", axis=1, tiled=True)
    hessian_panel = lax.psum(partial_panel, "tok") / total_count
    block = lax.all_gather(hessian_panel[:panel_width], "col", axis=0, tiled=True)
    rows = lax.broadcasted_iota(jnp.int32, (B, B), 0)
    columns = lax.broadcasted_iota(jnp.int32, (B, B), 1)
    on_diagonal = rows == columns
    mean_diagonal = jnp.sum(jnp.where(on_diagonal, block, 0.0)) / B
    damped = block + jnp.where(on_diagonal, 0.01 * mean_diagonal, 0.0)
    scale = lax.rsqrt(jnp.sum(damped * damped))
    g = damped * scale
    y = pruned_panel.astype(jnp.float32)
    for sweep in range(ITERS):
        g_high = g.astype(jnp.bfloat16)
        y_high, y_low = split(y)
        y = 2.0 * y - (mm(y_high, g_high) + mm(y_low, g_high))
        if sweep < ITERS - 1:
            g = 2.0 * g - mm(g_high, g_high)
    y_high, y_low = split(y * scale)
    h_high, h_low = split(hessian_panel)
    nt = (((1,), (1,)), ((), ()))
    correction = mm(y_high, h_high, nt) + mm(y_low, h_high, nt) + mm(y_high, h_low, nt)
    kept = keep_mask.astype(jnp.float32)
    return (kept * (weight.astype(jnp.float32) - correction)).astype(jnp.bfloat16)


def solution(mesh):
    return jax.shard_map(
        per_device,
        mesh=mesh,
        in_specs=(P("tok", "col"), P("tok", "col"), P("tok", "col")),
        out_specs=P("tok", "col"),
        check_vma=False,
    )
```

profile of v0, /device:TPU:1, one launch (start us, length us, event | category | flops | bytes accessed | tf_op | source)
XLA Modules:
  0.0 284.6 jit_solution(3406045359667828655)
XLA Ops:
  6.5 1.2 slice.14
  7.8 0.9 copy.10
  8.7 46.8 %all-gather.6.cloned.1.call-done = bf16[2048,1024]{0,1:T(8,128)(2,1)} async-done(((bf16[2048,64]{0,1:T(8,128)(2,1)}), bf16[2048,1024]{0,1:T(8,128)(2,1)}) %all-gather.6.cloned.1.call-update) | async-done | bytes 4194320 | tf_op jit(solution)/shard_map/all_gather | solution.py:28
  55.6 5.9 %fusion.29 = f32[512,1024]{1,0:T(8,128)} fusion(bf16[2048,512]{1,0:T(8,128)(2,1)S(1)} %copy-done.4, bf16[2048,1024]{0,1:T(8,128)(2,1)} %all-gather.6.cloned.1.call-done), kind=kOutput, calls=%fused_computation.50 | convolution fusion | flops 2147483648 | bytes 8388608 | tf_op jit(solution)/shard_map/dot_general | solution.py:16
  61.5 0.8 slice-done.1
  63.3 95.8 %all-reduce.2.cloned.1.call-done = f32[512,1024]{1,0:T(8,128)} async-done(((f32[512,1024]{1,0:T(8,128)}), f32[512,1024]{1,0:T(8,128)}) %all-reduce.2.cloned.1.call-update) | async-done | bytes 2097168 | tf_op jit(solution)/shard_map/psum | solution.py:31
  159.1 1.8 broadcast_multiply_fusion
  161.6 39.0 %all-gather.4.cloned.1.call-done = bf16[512,1024]{0,1:T(8,128)(2,1)} async-done(((bf16[512,64]{0,1:T(8,128)(2,1)}), bf16[512,1024]{0,1:T(8,128)(2,1)}) %all-gather.4.cloned.1.call-update) | async-done | bytes 1048592 | tf_op jit(solution)/shard_map/all_gather | solution.py:30
  200.6 1.7 copy.6
  202.3 41.0 %all-gather.8.cloned.1.call-done = f32[1024,1024]{1,0:T(8,128)} async-done(((f32[64,1024]{1,0:T(8,128)}), f32[1024,1024]{1,0:T(8,128)}) %all-gather.8.cloned.1.call-update) | async-done | bytes 4194320 | tf_op jit(solution)/shard_map/all_gather | solution.py:32
  243.3 2.9 %select_reduce_fusion = f32[]{:T(128)} fusion(f32[1024,1024]{1,0:T(8,128)} %all-gather.8.cloned.1.call-done), kind=kLoop, calls=%fused_computation.5 | loop fusion | flops 3145727 | bytes 4194308 | tf_op jit(solution)/shard_map/reduce_sum | solution.py:36
  246.9 3.9 %multiply_reduce_fusion = f32[]{:T(128)} fusion(f32[1024,1024]{1,0:T(8,128)} %all-gather.8.cloned.1.call-done, f32[]{:T(128)S(6)} %mul_shard_map.3), kind=kLoop, calls=%fused_computation.3 | loop fusion | flops 5242879 | bytes 4194312 | tf_op jit(solution)/shard_map/reduce_sum | solution.py:38
  251.4 7.0 %multiply_subtract_fusion.1 = f32[1024,1024]{1,0:T(8,128)S(1)} fusion(f32[1024,1024]{1,0:T(8,128)} %all-gather.8.cloned.1.call-done, f32[]{:T(128)S(6)} %rsqrt.3, f32[]{:T(128)S(6)} %mul_shard_map.3), kind=kOutput, calls=%fused_computation.2 | convolution fusion | flops 2159017984 | bytes 8388616 | tf_op jit(solution)/shard_map/dot_general | solution.py:16
  258.5 2.3 multiply_subtract_fusion
  260.8 1.3 fusion.20
  262.1 1.4 fusion.6
  263.5 1.3 fusion.17
  264.8 1.3 add_subtract_fusion.1
  266.2 2.4 subtract_convert_fusion
  268.5 1.3 fusion.18
  269.8 1.6 add_subtract_fusion
  271.5 1.3 fusion.19
  272.7 1.4 subtract_multiply_fusion
  276.4 1.6 fusion.10
  (27 shorter events, 4.1 us)
Async XLA Ops:
  6.5 49.0 %copy-start.4 = (bf16[2048,512]{1,0:T(8,128)(2,1)S(1)}, bf16[2048,512]{1,0:T(8,128)(2,1)}, u32[]{:S(2)}) copy-start(bf16[2048,512]{1,0:T(8,128)(2,1)} %param.3) | copy-start | bytes 6291460
  6.5 49.0 %all-gather.6.cloned.1.call-start = ((), (), s32[]{:S(2)}) async-start(), calls=%async_computation.1 | async-start | bytes 4456448 | tf_op jit(solution)/shard_map/all_gather | solution.py:28
  8.7 150.4 %all-reduce.2.cloned.1.call-start = ((), (), s32[]{:S(2)}) async-start(), calls=%async_computation.2 | async-start | bytes 4194304 | tf_op jit(solution)/shard_map/psum | solution.py:31
  61.5 0.9 slice-start.1
  61.5 1.0 slice-start
  61.5 139.1 %all-gather.4.cloned.1.call-start = ((), (), s32[]{:S(2)}) async-start(), calls=%async_computation | async-start | bytes 1114112 | tf_op jit(solution)/shard_map/all_gather | solution.py:30
  63.3 180.0 %all-gather.8.cloned.1.call-start = ((), (), s32[]{:S(2)}) async-start(), calls=%async_computation.3 | async-start | bytes 4456448 | tf_op jit(solution)/shard_map/all_gather | solution.py:32
  258.5 2.4 copy-start.1
  272.7 1.6 copy-start
  275.1 1.2 copy-start.2
  275.1 1.3 copy-start.3
Sparse Core Ops, SparseCore 0:
  9.2 46.3 all-gather.5
  61.6 97.4 all-reduce.1
  161.1 39.5 all-gather.3
  202.4 40.7 all-gather.7
where the time goes:
time: 285 us
  waiting for transfers between devices  223 us (78%)
  matrix products  31.6 us (11%)
  between operations  14.6 us (5%)
  other arithmetic  9.21 us (3%)
  local copies, waits for them, and re-layouts  6.38 us (2%)
    psum x1, waiting for transfers between devices, per_device(): hessian_panel = lax.psum(partial_panel, 'tok') / total_count  95.8 us
    all_gather x1, waiting for transfers between devices, per_device(): lax.all_gather(activations[:, :panel_width], 'col', axis=1, tiled=True)  46.8 us
    all_gather x1, waiting for transfers between devices, per_device(): lax.all_gather(hessian_panel[:panel_width], 'col', axis=0, tiled=True)  41 us
    all_gather x1, waiting for transfers between devices, per_device(): pruned_panel = lax.all_gather(pruned, 'col', axis=1, tiled=True)  39 us
    dot_general x15, matrix products, mm(): return lax.dot_general(a, b, dims, preferred_element_type=jnp.float32)  31.6 us
  transfers between devices with their start and end apart: 4, of which 4 were waited for; matrix products, arithmetic and copies ran while one was open for 2% of the time, Pallas kernels for 0%

commit v1 on v0

--- a/solution.py
+++ b/solution.py
@@ -5,6 +5,19 @@
 
 B = 1024
 ITERS = 4
+
+
+def collect(shard, axis, dim):
+    ways = lax.axis_size(axis)
+    up = [(d, (d + 1) % ways) for d in range(ways)]
+    down = [(d, (d - 1) % ways) for d in range(ways)]
+    earlier, later = ([shard], [shard])
+    for _ in range(ways // 2):
+        earlier.append(lax.ppermute(earlier[-1], axis, up))
+    for _ in range((ways - 1) // 2):
+        later.append(lax.ppermute(later[-1], axis, down))
+    line = jnp.concatenate([*earlier[::-1], *later[1:]], axis=dim)
+    return jnp.roll(line, (lax.axis_index(axis) - ways // 2) * shard.shape[dim], axis=dim)
 
 
 def split(x):
@@ -27,7 +40,7 @@
     )
     panel = lax.all_gather(activations[:, :panel_width], "col", axis=1, tiled=True)
     partial_panel = mm(activations, panel, (((0,), (0,)), ((), ())))
-    pruned_panel = lax.all_gather(pruned, "col", axis=1, tiled=True)
+    pruned_panel = collect(pruned, "col", 1)
     hessian_panel = lax.psum(partial_panel, "tok") / total_count
     block = lax.all_gather(hessian_panel[:panel_width], "col", axis=0, tiled=True)
     rows = lax.broadcasted_iota(jnp.int32, (B, B), 0)

time: 285 us -> 264 us (0.926)
  the two profiles are of different devices: /device:TPU:1 before, /device:TPU:6 now
where the time goes in v1:
time: 264 us
  waiting for transfers between devices  174 us (66%)
  matrix products  31.7 us (12%)
  starting transfers between devices  23.2 us (9%)
  between operations  14.7 us (6%)
  local copies, waits for them, and re-layouts  10.3 us (4%)
  other arithmetic  9.52 us (4%)
    psum x1, waiting for transfers between devices, per_device(): hessian_panel = lax.psum(partial_panel, 'tok') / total_count  98.8 us
    all_gather x1, waiting for transfers between devices, per_device(): lax.all_gather(activations[:, :panel_width], 'col', axis=1, tiled=True)  45.5 us
    dot_general x15, matrix products, mm(): return lax.dot_general(a, b, dims, preferred_element_type=jnp.float32)  31.7 us
    ppermute x7, starting transfers between devices, collect(): later.append(lax.ppermute(later[-1], axis, down))  23 us
    ppermute x7, waiting for transfers between devices, collect(): later.append(lax.ppermute(later[-1], axis, down))  19.4 us
    ppermute x8, waiting for transfers between devices, collect(): earlier.append(lax.ppermute(earlier[-1], axis, up))  10.4 us
    concatenate x1, local copies, waits for them, and re-layouts, collect(): jnp.roll(line, (lax.axis_index(axis) - ways // 2) * shard.shape[dim], axi...  6.23 us
  transfers between devices with their start and end apart: 18, of which 13 were waited for; matrix products, arithmetic and copies ran while one was open for 3% of the time, Pallas kernels for 0%

profile of v1, /device:TPU:6, one launch (start us, length us, event | category | flops | bytes accessed | tf_op | source)
XLA Modules:
  0.0 263.6 jit_solution(15248305475299800622)
XLA Ops:
  8.7 45.5 %all-gather.3.cloned.1.call-done = bf16[2048,1024]{0,1:T(8,128)(2,1)} async-done(((bf16[2048,64]{0,1:T(8,128)(2,1)}), bf16[2048,1024]{0,1:T(8,128)(2,1)}) %all-gather.3.cloned.1.call-update) | async-done | bytes 4194320 | tf_op jit(solution)/shard_map/all_gather | solution.py:41
  54.2 6.0 %fusion.34 = f32[512,1024]{1,0:T(8,128)} fusion(bf16[2048,512]{1,0:T(8,128)(2,1)S(1)} %copy-done.16, bf16[2048,1024]{0,1:T(8,128)(2,1)} %all-gather.3.cloned.1.call-done), kind=kOutput, calls=%fused_computation.55 | convolution fusion | flops 2147483648 | bytes 8388608 | tf_op jit(solution)/shard_map/dot_general | solution.py:29
  60.3 98.8 %all-reduce.2.cloned.1.call-done = f32[512,1024]{1,0:T(8,128)} async-done(((f32[512,1024]{1,0:T(8,128)}), f32[512,1024]{1,0:T(8,128)}) %all-reduce.2.cloned.1.call-update) | async-done | bytes 2097168 | tf_op jit(solution)/shard_map/psum | solution.py:44
  162.5 2.9 %collective-permute-start.8 = (bf16[512,64]{1,0:T(8,128)(2,1)S(1)}, bf16[512,64]{1,0:T(8,128)(2,1)S(1)}, u32[]{:S(2)}, u32[]{:S(2)}) collective-permute-start(bf16[512,64]{1,0:T(8,128)(2,1)S(1)} %fusion.25), channel_id=1, source_target_pairs={{0,15},{1,0},{2,1},{3,2},{4,3},{5,4},{6,5},{7,6},{8,7},{9,8},{10,9... | collective-permute-start | bytes 196616 | tf_op jit(solution)/shard_map/ppermute | solution.py:18
  165.5 2.6 %collective-permute-done = bf16[512,64]{1,0:T(8,128)(2,1)S(1)} collective-permute-done((bf16[512,64]{1,0:T(8,128)(2,1)S(1)}, bf16[512,64]{1,0:T(8,128)(2,1)S(1)}, u32[]{:S(2)}, u32[]{:S(2)}) %collective-permute-start) | collective-permute-done | bytes 65568 | tf_op jit(solution)/shard_map/ppermute | solution.py:16
  168.1 3.0 %collective-permute-start.9 = (bf16[512,64]{1,0:T(8,128)(2,1)S(1)}, bf16[512,64]{1,0:T(8,128)(2,1)S(1)}, u32[]{:S(2)}, u32[]{:S(2)}) collective-permute-start(bf16[512,64]{1,0:T(8,128)(2,1)S(1)} %collective-permute-done.8), channel_id=1, source_target_pairs={{0,15},{1,0},{2,1},{3,2},{4,3},{5,4},{6,5},{7,6},{8,7},{9,8},{10,9... | collective-permute-start | bytes 196616 | tf_op jit(solution)/shard_map/ppermute | solution.py:18
  171.1 2.6 %collective-permute-done.1 = bf16[512,64]{1,0:T(8,128)(2,1)S(1)} collective-permute-done((bf16[512,64]{1,0:T(8,128)(2,1)S(1)}, bf16[512,64]{1,0:T(8,128)(2,1)S(1)}, u32[]{:S(2)}, u32[]{:S(2)}) %collective-permute-start.1) | collective-permute-done | bytes 65568 | tf_op jit(solution)/shard_map/ppermute | solution.py:16
  175.8 3.5 %collective-permute-start.10 = (bf16[512,64]{1,0:T(8,128)(2,1)S(1)}, bf16[512,64]{1,0:T(8,128)(2,1)S(1)}, u32[]{:S(2)}, u32[]{:S(2)}) collective-permute-start(bf16[512,64]{1,0:T(8,128)(2,1)S(1)} %collective-permute-done.9), channel_id=1, source_target_pairs={{0,15},{1,0},{2,1},{3,2},{4,3},{5,4},{6,5},{7,6},{8,7},{9,8},{10,9... | collective-permute-start | bytes 196616 | tf_op jit(solution)/shard_map/ppermute | solution.py:18
  181.4 2.8 %collective-permute-done.10 = bf16[512,64]{1,0:T(8,128)(2,1)S(1)} collective-permute-done((bf16[512,64]{1,0:T(8,128)(2,1)S(1)}, bf16[512,64]{1,0:T(8,128)(2,1)S(1)}, u32[]{:S(2)}, u32[]{:S(2)}) %collective-permute-start.10) | collective-permute-done | bytes 65568 | tf_op jit(solution)/shard_map/ppermute | solution.py:18
  184.2 3.5 %collective-permute-start.11 = (bf16[512,64]{1,0:T(8,128)(2,1)S(1)}, bf16[512,64]{1,0:T(8,128)(2,1)S(1)}, u32[]{:S(2)}, u32[]{:S(2)}) collective-permute-start(bf16[512,64]{1,0:T(8,128)(2,1)S(1)} %collective-permute-done.10), channel_id=1, source_target_pairs={{0,15},{1,0},{2,1},{3,2},{4,3},{5,4},{6,5},{7,6},{8,7},{9,8},{10,9... | collective-permute-start | bytes 196616 | tf_op jit(solution)/shard_map/ppermute | solution.py:18
  188.2 4.6 %collective-permute-done.11 = bf16[512,64]{1,0:T(8,128)(2,1)S(1)} collective-permute-done((bf16[512,64]{1,0:T(8,128)(2,1)S(1)}, bf16[512,64]{1,0:T(8,128)(2,1)S(1)}, u32[]{:S(2)}, u32[]{:S(2)}) %collective-permute-start.11) | collective-permute-done | bytes 65568 | tf_op jit(solution)/shard_map/ppermute | solution.py:18
  192.9 3.5 %collective-permute-start.12 = (bf16[512,64]{1,0:T(8,128)(2,1)S(1)}, bf16[512,64]{1,0:T(8,128)(2,1)S(1)}, u32[]{:S(2)}, u32[]{:S(2)}) collective-permute-start(bf16[512,64]{1,0:T(8,128)(2,1)S(1)} %collective-permute-done.11), channel_id=1, source_target_pairs={{0,15},{1,0},{2,1},{3,2},{4,3},{5,4},{6,5},{7,6},{8,7},{9,8},{10,9... | collective-permute-start | bytes 196616 | tf_op jit(solution)/shard_map/ppermute | solution.py:18
  196.4 5.0 %collective-permute-done.12 = bf16[512,64]{1,0:T(8,128)(2,1)S(1)} collective-permute-done((bf16[512,64]{1,0:T(8,128)(2,1)S(1)}, bf16[512,64]{1,0:T(8,128)(2,1)S(1)}, u32[]{:S(2)}, u32[]{:S(2)}) %collective-permute-start.12) | collective-permute-done | bytes 65568 | tf_op jit(solution)/shard_map/ppermute | solution.py:18
  201.4 3.5 %collective-permute-start.13 = (bf16[512,64]{1,0:T(8,128)(2,1)S(1)}, bf16[512,64]{1,0:T(8,128)(2,1)S(1)}, u32[]{:S(2)}, u32[]{:S(2)}) collective-permute-start(bf16[512,64]{1,0:T(8,128)(2,1)S(1)} %collective-permute-done.12), channel_id=1, source_target_pairs={{0,15},{1,0},{2,1},{3,2},{4,3},{5,4},{6,5},{7,6},{8,7},{9,8},{10,9... | collective-permute-start | bytes 196616 | tf_op jit(solution)/shard_map/ppermute | solution.py:18
  204.9 2.5 collective-permute-done.13
  207.4 3.1 %collective-permute-start.14 = (bf16[512,64]{1,0:T(8,128)(2,1)S(1)}, bf16[512,64]{1,0:T(8,128)(2,1)S(1)}, u32[]{:S(2)}, u32[]{:S(2)}) collective-permute-start(bf16[512,64]{1,0:T(8,128)(2,1)S(1)} %collective-permute-done.13), channel_id=1, source_target_pairs={{0,15},{1,0},{2,1},{3,2},{4,3},{5,4},{6,5},{7,6},{8,7},{9,8},{10,9... | collective-permute-start | bytes 196616 | tf_op jit(solution)/shard_map/ppermute | solution.py:18
  210.5 2.5 collective-permute-done.14
  213.7 2.5 collective-permute-done.7
  216.2 6.2 %concatenate.6 = bf16[512,2048]{1,0:T(8,128)(2,1)S(1)} concatenate(bf16[512,64]{1,0:T(8,128)(2,1)} %collective-permute-done.7, bf16[512,64]{1,0:T(8,128)(2,1)} %copy-done.14, bf16[512,64]{1,0:T(8,128)(2,1)} %copy-done.12, bf16[512,64]{1,0:T(8,128)(2,1)} %copy-done.10, bf16[512,64]{1,0:T(8,128)(2,1)} %copy-done.8, bf16[512,64]{1,0:T(8,128)(2,1)} %copy-done.6, ...), dimensions={1} | concatenate | bytes 4194304 | tf_op jit(solution)/shard_map/jit(_roll_dynamic)/concatenate | solution.py:20
  222.5 2.9 %select_reduce_fusion = f32[]{:T(128)} fusion(f32[1024,1024]{1,0:T(8,128)} %all-gather.5.cloned.1.call-done), kind=kLoop, calls=%fused_computation.5 | loop fusion | flops 3145727 | bytes 4194308 | tf_op jit(solution)/shard_map/reduce_sum | solution.py:49
  226.1 3.9 %multiply_reduce_fusion = f32[]{:T(128)} fusion(f32[1024,1024]{1,0:T(8,128)} %all-gather.5.cloned.1.call-done, f32[]{:T(128)S(6)} %mul_shard_map.3), kind=kLoop, calls=%fused_computation.3 | loop fusion | flops 5242879 | bytes 4194312 | tf_op jit(solution)/shard_map/reduce_sum | solution.py:51
  230.6 7.1 %multiply_subtract_fusion.1 = f32[1024,1024]{1,0:T(8,128)S(1)} fusion(f32[1024,1024]{1,0:T(8,128)} %all-gather.5.cloned.1.call-done, f32[]{:T(128)S(6)} %rsqrt.3, f32[]{:T(128)S(6)} %mul_shard_map.3), kind=kOutput, calls=%fused_computation.2 | convolution fusion | flops 2159017984 | bytes 8388616 | tf_op jit(solution)/shard_map/dot_general | solution.py:29
  237.8 2.4 multiply_subtract_fusion
  245.6 2.4 subtract_convert_fusion
  (72 shorter events, 25.6 us)
Async XLA Ops:
  6.5 47.7 %copy-start.16 = (bf16[2048,512]{1,0:T(8,128)(2,1)S(1)}, bf16[2048,512]{1,0:T(8,128)(2,1)}, u32[]{:S(2)}) copy-start(bf16[2048,512]{1,0:T(8,128)(2,1)} %param.3) | copy-start | bytes 6291460
  6.5 47.7 %all-gather.3.cloned.1.call-start = ((), (), s32[]{:S(2)}) async-start(), calls=%async_computation | async-start | bytes 4456448 | tf_op jit(solution)/shard_map/all_gather | solution.py:41
  8.7 150.4 %all-reduce.2.cloned.1.call-start = ((), (), s32[]{:S(2)}) async-start(), calls=%async_computation.1 | async-start | bytes 4194304 | tf_op jit(solution)/shard_map/psum | solution.py:44
  60.2 101.3 %copy-start.2 = (s32[512,512]{1,0:T(8,128)S(1)}, s32[512,512]{1,0:T(8,128)}, u32[]{:S(2)}) copy-start(s32[512,512]{1,0:T(8,128)} %param.5) | copy-start | bytes 3145732
  60.2 162.3 %all-gather.5.cloned.1.call-start = ((), (), s32[]{:S(2)}) async-start(), calls=%async_computation.2 | async-start | bytes 4456448 | tf_op jit(solution)/shard_map/all_gather | solution.py:45
  162.5 5.6 %collective-permute-start = (bf16[512,64]{1,0:T(8,128)(2,1)S(1)}, bf16[512,64]{1,0:T(8,128)(2,1)S(1)}, u32[]{:S(2)}, u32[]{:S(2)}) collective-permute-start(bf16[512,64]{1,0:T(8,128)(2,1)S(1)} %fusion.25), channel_id=1, source_target_pairs={{0,1},{1,2},{2,3},{3,4},{4,5},{5,6},{6,7},{7,8},{8,9},{9,10},{10,1... | collective-permute-start | bytes 196616 | tf_op jit(solution)/shard_map/ppermute | solution.py:16
  162.5 5.6 %collective-permute-start.8 = (bf16[512,64]{1,0:T(8,128)(2,1)S(1)}, bf16[512,64]{1,0:T(8,128)(2,1)S(1)}, u32[]{:S(2)}, u32[]{:S(2)}) collective-permute-start(bf16[512,64]{1,0:T(8,128)(2,1)S(1)} %fusion.25), channel_id=1, source_target_pairs={{0,15},{1,0},{2,1},{3,2},{4,3},{5,4},{6,5},{7,6},{8,7},{9,8},{10,9... | collective-permute-start | bytes 196616 | tf_op jit(solution)/shard_map/ppermute | solution.py:18
  168.1 5.6 %collective-permute-start.1 = (bf16[512,64]{1,0:T(8,128)(2,1)S(1)}, bf16[512,64]{1,0:T(8,128)(2,1)S(1)}, u32[]{:S(2)}, u32[]{:S(2)}) collective-permute-start(bf16[512,64]{1,0:T(8,128)(2,1)S(1)} %collective-permute-done), channel_id=1, source_target_pairs={{0,1},{1,2},{2,3},{3,4},{4,5},{5,6},{6,7},{7,8},{8,9},{9,10},{10,1... | collective-permute-start | bytes 196616 | tf_op jit(solution)/shard_map/ppermute | solution.py:16
  168.1 7.6 %collective-permute-start.9 = (bf16[512,64]{1,0:T(8,128)(2,1)S(1)}, bf16[512,64]{1,0:T(8,128)(2,1)S(1)}, u32[]{:S(2)}, u32[]{:S(2)}) collective-permute-start(bf16[512,64]{1,0:T(8,128)(2,1)S(1)} %collective-permute-done.8), channel_id=1, source_target_pairs={{0,15},{1,0},{2,1},{3,2},{4,3},{5,4},{6,5},{7,6},{8,7},{9,8},{10,9... | collective-permute-start | bytes 196616 | tf_op jit(solution)/shard_map/ppermute | solution.py:18
  173.7 7.7 %collective-permute-start.2 = (bf16[512,64]{1,0:T(8,128)(2,1)S(1)}, bf16[512,64]{1,0:T(8,128)(2,1)S(1)}, u32[]{:S(2)}, u32[]{:S(2)}) collective-permute-start(bf16[512,64]{1,0:T(8,128)(2,1)S(1)} %collective-permute-done.1), channel_id=1, source_target_pairs={{0,1},{1,2},{2,3},{3,4},{4,5},{5,6},{6,7},{7,8},{8,9},{9,10},{10,1... | collective-permute-start | bytes 196616 | tf_op jit(solution)/shard_map/ppermute | solution.py:16
  175.8 5.6 %copy-start.5 = (bf16[512,64]{1,0:T(8,128)(2,1)}, bf16[512,64]{1,0:T(8,128)(2,1)S(1)}, u32[]{:S(2)}) copy-start(bf16[512,64]{1,0:T(8,128)(2,1)S(1)} %collective-permute-done.9) | copy-start | bytes 196612
  175.8 8.4 %collective-permute-start.10 = (bf16[512,64]{1,0:T(8,128)(2,1)S(1)}, bf16[512,64]{1,0:T(8,128)(2,1)S(1)}, u32[]{:S(2)}, u32[]{:S(2)}) collective-permute-start(bf16[512,64]{1,0:T(8,128)(2,1)S(1)} %collective-permute-done.9), channel_id=1, source_target_pairs={{0,15},{1,0},{2,1},{3,2},{4,3},{5,4},{6,5},{7,6},{8,7},{9,8},{10,9... | collective-permute-start | bytes 196616 | tf_op jit(solution)/shard_map/ppermute | solution.py:18
  181.4 6.8 %collective-permute-start.3 = (bf16[512,64]{1,0:T(8,128)(2,1)S(1)}, bf16[512,64]{1,0:T(8,128)(2,1)S(1)}, u32[]{:S(2)}, u32[]{:S(2)}) collective-permute-start(bf16[512,64]{1,0:T(8,128)(2,1)S(1)} %collective-permute-done.2), channel_id=1, source_target_pairs={{0,1},{1,2},{2,3},{3,4},{4,5},{5,6},{6,7},{7,8},{8,9},{9,10},{10,1... | collective-permute-start | bytes 196616 | tf_op jit(solution)/shard_map/ppermute | solution.py:16
  184.2 8.7 %collective-permute-start.11 = (bf16[512,64]{1,0:T(8,128)(2,1)S(1)}, bf16[512,64]{1,0:T(8,128)(2,1)S(1)}, u32[]{:S(2)}, u32[]{:S(2)}) collective-permute-start(bf16[512,64]{1,0:T(8,128)(2,1)S(1)} %collective-permute-done.10), channel_id=1, source_target_pairs={{0,15},{1,0},{2,1},{3,2},{4,3},{5,4},{6,5},{7,6},{8,7},{9,8},{10,9... | collective-permute-start | bytes 196616 | tf_op jit(solution)/shard_map/ppermute | solution.py:18
  188.2 4.7 %copy-start.8 = (bf16[512,64]{1,0:T(8,128)(2,1)}, bf16[512,64]{1,0:T(8,128)(2,1)S(1)}, u32[]{:S(2)}) copy-start(bf16[512,64]{1,0:T(8,128)(2,1)S(1)} %collective-permute-done.3) | copy-start | bytes 196612
  188.2 8.2 %collective-permute-start.4 = (bf16[512,64]{1,0:T(8,128)(2,1)S(1)}, bf16[512,64]{1,0:T(8,128)(2,1)S(1)}, u32[]{:S(2)}, u32[]{:S(2)}) collective-permute-start(bf16[512,64]{1,0:T(8,128)(2,1)S(1)} %collective-permute-done.3), channel_id=1, source_target_pairs={{0,1},{1,2},{2,3},{3,4},{4,5},{5,6},{6,7},{7,8},{8,9},{9,10},{10,1... | collective-permute-start | bytes 196616 | tf_op jit(solution)/shard_map/ppermute | solution.py:16
  192.9 8.5 %collective-permute-start.12 = (bf16[512,64]{1,0:T(8,128)(2,1)S(1)}, bf16[512,64]{1,0:T(8,128)(2,1)S(1)}, u32[]{:S(2)}, u32[]{:S(2)}) collective-permute-start(bf16[512,64]{1,0:T(8,128)(2,1)S(1)} %collective-permute-done.11), channel_id=1, source_target_pairs={{0,15},{1,0},{2,1},{3,2},{4,3},{5,4},{6,5},{7,6},{8,7},{9,8},{10,9... | collective-permute-start | bytes 196616 | tf_op jit(solution)/shard_map/ppermute | solution.py:18
  196.4 5.0 %copy-start.10 = (bf16[512,64]{1,0:T(8,128)(2,1)}, bf16[512,64]{1,0:T(8,128)(2,1)S(1)}, u32[]{:S(2)}) copy-start(bf16[512,64]{1,0:T(8,128)(2,1)S(1)} %collective-permute-done.4) | copy-start | bytes 196612
  196.4 8.5 %collective-permute-start.5 = (bf16[512,64]{1,0:T(8,128)(2,1)S(1)}, bf16[512,64]{1,0:T(8,128)(2,1)S(1)}, u32[]{:S(2)}, u32[]{:S(2)}) collective-permute-start(bf16[512,64]{1,0:T(8,128)(2,1)S(1)} %collective-permute-done.4), channel_id=1, source_target_pairs={{0,1},{1,2},{2,3},{3,4},{4,5},{5,6},{6,7},{7,8},{8,9},{9,10},{10,1... | collective-permute-start | bytes 196616 | tf_op jit(solution)/shard_map/ppermute | solution.py:16
  201.4 6.0 %collective-permute-start.13 = (bf16[512,64]{1,0:T(8,128)(2,1)S(1)}, bf16[512,64]{1,0:T(8,128)(2,1)S(1)}, u32[]{:S(2)}, u32[]{:S(2)}) collective-permute-start(bf16[512,64]{1,0:T(8,128)(2,1)S(1)} %collective-permute-done.12), channel_id=1, source_target_pairs={{0,15},{1,0},{2,1},{3,2},{4,3},{5,4},{6,5},{7,6},{8,7},{9,8},{10,9... | collective-permute-start | bytes 196616 | tf_op jit(solution)/shard_map/ppermute | solution.py:18
  204.9 5.6 %collective-permute-start.6 = (bf16[512,64]{1,0:T(8,128)(2,1)S(1)}, bf16[512,64]{1,0:T(8,128)(2,1)S(1)}, u32[]{:S(2)}, u32[]{:S(2)}) collective-permute-start(bf16[512,64]{1,0:T(8,128)(2,1)S(1)} %collective-permute-done.5), channel_id=1, source_target_pairs={{0,1},{1,2},{2,3},{3,4},{4,5},{5,6},{6,7},{7,8},{8,9},{9,10},{10,1... | collective-permute-start | bytes 196616 | tf_op jit(solution)/shard_map/ppermute | solution.py:16
  207.4 5.6 %copy-start.13 = (bf16[512,64]{1,0:T(8,128)(2,1)}, bf16[512,64]{1,0:T(8,128)(2,1)S(1)}, u32[]{:S(2)}) copy-start(bf16[512,64]{1,0:T(8,128)(2,1)S(1)} %collective-permute-done.13) | copy-start | bytes 196612
  207.4 5.6 %collective-permute-start.14 = (bf16[512,64]{1,0:T(8,128)(2,1)S(1)}, bf16[512,64]{1,0:T(8,128)(2,1)S(1)}, u32[]{:S(2)}, u32[]{:S(2)}) collective-permute-start(bf16[512,64]{1,0:T(8,128)(2,1)S(1)} %collective-permute-done.13), channel_id=1, source_target_pairs={{0,15},{1,0},{2,1},{3,2},{4,3},{5,4},{6,5},{7,6},{8,7},{9,8},{10,9... | collective-permute-start | bytes 196616 | tf_op jit(solution)/shard_map/ppermute | solution.py:18
  210.5 5.7 %collective-permute-start.7 = (bf16[512,64]{1,0:T(8,128)(2,1)S(1)}, bf16[512,64]{1,0:T(8,128)(2,1)}, u32[]{:S(2)}, u32[]{:S(2)}) collective-permute-start(bf16[512,64]{1,0:T(8,128)(2,1)S(1)} %collective-permute-done.6), channel_id=1, source_target_pairs={{0,1},{1,2},{2,3},{3,4},{4,5},{5,6},{6,7},{7,8},{8,9},{9,10},{10,1... | collective-permute-start | bytes 196616 | tf_op jit(solution)/shard_map/ppermute | solution.py:16
  (11 other events, 26.6 us)
Sparse Core Ops, SparseCore 0:
  9.2 45.0 all-gather.2
  60.3 98.6 all-reduce.1
  161.7 44.6 all-gather.4
